TPU v7x, 32 devices: a whole 2x2x4 slice. The times are simulated.
32 devices in a mesh: dp: 16 (over z, x, core), head: 2 (over y).
Axes of the slice: x: 2, y: 2, z: 4, core: 2. Of those that a mesh axis runs over, the one named last changes fastest.
Arguments:
- tokens: bfloat16 [32768, 512], P(('dp', 'head')), may hold values from -6 to 6
- lengths: int32 [128], P('dp'), may hold values from 40 to 256, as said below
- ln1_gain: float32 [512], replicated, may hold values from 0.5 to 1.5
- ln1_bias: float32 [512], replicated, may hold values from -1 to 1
- w_query: bfloat16 [512, 512], P(None, 'head'), may hold values from -0.25 to 0.25
- w_key: bfloat16 [512, 512], P(None, 'head'), may hold values from -0.25 to 0.25
- w_value: bfloat16 [512, 512], P(None, 'head'), may hold values from -0.25 to 0.25
- w_out: bfloat16 [512, 512], P('head'), may hold values from -1 to 1
- sort_first: bfloat16 [512, 512], replicated, may hold values from -0.25 to 0.25
- sort_second: bfloat16 [512, 8], replicated, may hold values from -0.5 to 0.5
- ln2_gain: float32 [512], replicated, may hold values from 0.5 to 1.5
- ln2_bias: float32 [512], replicated, may hold values from -1 to 1
- w_up: bfloat16 [512, 2048], replicated, may hold values from -0.25 to 0.25
- w_down: bfloat16 [2048, 512], replicated, may hold values from -0.125 to 0.125
- cotangent: bfloat16 [32768, 512], P(('dp', 'head')), may hold values from -6 to 6
Outputs:
- output: bfloat16 [32768, 512], P(('dp', 'head'))
- input_grad: bfloat16 [32768, 512], P(('dp', 'head'))
- grad_ln1_gain: float32 [512], replicated
- grad_ln1_bias: float32 [512], replicated
- grad_query: float32 [512, 512], P(None, 'head')
- grad_key: float32 [512, 512], P(None, 'head')
- grad_value: float32 [512, 512], P(None, 'head')
- grad_out: float32 [512, 512], P('head')
- grad_sort_first: float32 [512, 512], replicated
- grad_sort_second: float32 [512, 8], replicated
- grad_ln2_gain: float32 [512], replicated
- grad_ln2_bias: float32 [512], replicated
- grad_up: float32 [512, 2048], replicated
- grad_down: float32 [2048, 512], replicated
Inputs may be any that keep to these rules, and one draw needn't show every extreme that they name: `lengths`: some sequence has exactly 256 valid tokens and some has exactly 40.
All inputs are finite; a program needn't handle non-finite values.
Results may differ from a plain program's by a relative error of at most 0.017.
Values may be sent and summed in bfloat16 or wider, within the bound.
No kernel may reach another device: no remote copies, remote signals or barrier semaphores. Data moves between devices by JAX's collectives and lax.ppermute only.
A program may use at most 192 MiB of HBM per device.

v0:
```python
import jax
import jax.numpy as jnp
from jax import lax
from jax.sharding import PartitionSpec as P

HD = 64
BL = 32
ITERS = 8
LMAX = 256
precise = lax.Precision.HIGHEST


def smooth_gate(values):
    return jax.nn.gelu(values, approximate=False)


def layer_norm(values, gain_vec, bias_vec):
    center = values - jnp.mean(values, axis=-1, keepdims=True)
    spread = jnp.mean(center * center, axis=-1, keepdims=True)
    return center * lax.rsqrt(spread + 1e-05) * gain_vec + bias_vec


def log_total(values, along):
    row_top = jnp.max(values, axis=along, keepdims=True)
    return row_top + jnp.log(jnp.sum(jnp.exp(values - row_top), axis=along, keepdims=True))


def sort_plan(summary, sort_one, sort_two, block_ok):
    hidden = smooth_gate(jnp.einsum("cid,de->cie", summary, sort_one, precision=precise))
    logits = jnp.einsum("cie,ej->cij", hidden, sort_two, precision=precise)
    diagonal = jnp.eye(logits.shape[1], dtype=jnp.bool_)[None]
    allowed = block_ok[:, :, None] & block_ok[:, None, :] | diagonal & ~block_ok[:, :, None]
    plan_log = jnp.where(allowed, logits, -1e30)
    for sweep_index in range(ITERS):
        plan_log = plan_log - log_total(plan_log, 2)
        plan_log = plan_log - log_total(plan_log, 1)
    return jnp.exp(plan_log)


def outer_product(left, right):
    return lax.dot_general(
        left, right, (((0,), (0,)), ((), ())), preferred_element_type=jnp.float32
    )


def attend_forward(queries, key_rows, value_rows, soft_plan, tok_ok, block_ok):
    tok_mask = tok_ok[..., None, None].astype(jnp.bfloat16)
    key_kept = key_rows * tok_mask
    value_kept = value_rows * tok_mask
    sorted_keys = jnp.einsum(
        "cij,cjthd->cithd", soft_plan, key_kept.astype(jnp.float32), precision=precise
    ).astype(jnp.bfloat16)
    sorted_values = jnp.einsum(
        "cij,cjthd->cithd", soft_plan, value_kept.astype(jnp.float32), precision=precise
    ).astype(jnp.bfloat16)
    all_keys = jnp.concatenate([key_kept, sorted_keys], axis=2)
    all_values = jnp.concatenate([value_kept, sorted_values], axis=2)
    score_scale = queries.shape[-1] ** (-0.5)
    scores = (
        jnp.einsum("cibhd,cikhd->cihbk", queries, all_keys, preferred_element_type=jnp.float32)
        * score_scale
    )
    key_ok = jnp.concatenate([tok_ok, jnp.broadcast_to(block_ok[:, :, None], tok_ok.shape)], axis=2)
    allowed = key_ok[:, :, None, None, :] | ~tok_ok[:, :, None, :, None]
    scores = jnp.where(allowed, scores, -1e30)
    weights = jnp.exp(scores - log_total(scores, 4))
    weights_low = weights.astype(jnp.bfloat16)
    mixed_rows = jnp.einsum(
        "cihbk,cikhd->cibhd", weights_low, all_values, preferred_element_type=jnp.float32
    )
    mixed_rows = mixed_rows * tok_ok[..., None, None].astype(jnp.float32)
    return (mixed_rows, (key_kept, all_keys, all_values, weights, weights_low))


def attend_backward(grad_mixed, queries, soft_plan, tok_ok, saved_state):
    key_kept, all_keys, all_values, weights, weights_low = saved_state
    block_len = key_kept.shape[2]
    score_scale = queries.shape[-1] ** (-0.5)
    value_kept = all_values[:, :, :block_len]
    grad_rows = grad_mixed * tok_ok[..., None, None].astype(jnp.bfloat16)
    grad_weights = jnp.einsum(
        "cibhd,cikhd->cihbk", grad_rows, all_values, preferred_element_type=jnp.float32
    )
    grad_all_values = jnp.einsum(
        "cihbk,cibhd->cikhd", weights_low, grad_rows, preferred_element_type=jnp.float32
    )
    weighted = jnp.sum(weights * grad_weights, axis=4, keepdims=True)
    grad_scores = (weights * (grad_weights - weighted)).astype(jnp.bfloat16)
    grad_queries = (
        jnp.einsum("cihbk,cikhd->cibhd", grad_scores, all_keys, preferred_element_type=jnp.float32)
        * score_scale
    )
    grad_all_keys = (
        jnp.einsum("cihbk,cibhd->cikhd", grad_scores, queries, preferred_element_type=jnp.float32)
        * score_scale
    )
    grad_sorted_keys = grad_all_keys[:, :, block_len:]
    grad_sorted_values = grad_all_values[:, :, block_len:]
    grad_plan = jnp.einsum(
        "cithd,cjthd->cij", grad_sorted_keys, key_kept.astype(jnp.float32), precision=precise
    )
    grad_plan = grad_plan + jnp.einsum(
        "cithd,cjthd->cij", grad_sorted_values, value_kept.astype(jnp.float32), precision=precise
    )
    key_total = grad_all_keys[:, :, :block_len] + jnp.einsum(
        "cij,cithd->cjthd", soft_plan, grad_sorted_keys, precision=precise
    )
    value_total = grad_all_values[:, :, :block_len] + jnp.einsum(
        "cij,cithd->cjthd", soft_plan, grad_sorted_values, precision=precise
    )
    tok_mask = tok_ok[..., None, None].astype(jnp.float32)
    return (
        grad_queries.astype(jnp.bfloat16),
        (key_total * tok_mask).astype(jnp.bfloat16),
        (value_total * tok_mask).astype(jnp.bfloat16),
        grad_plan,
    )


def run_attention(normed_here, span_list, query_cols, key_cols, value_cols, sort_one, sort_two):
    seq_count = span_list.shape[0]
    nblocks = LMAX // BL
    heads_here = query_cols.shape[1] // HD
    positions = jnp.arange(LMAX, dtype=jnp.int32)
    tok_ok = (positions[None, :] < span_list[:, None]).reshape(seq_count, nblocks, BL)
    block_ok = (jnp.arange(nblocks, dtype=jnp.int32) * BL)[None, :] < span_list[:, None]
    block_shape = (seq_count, nblocks, BL, heads_here, HD)
    queries = (
        jnp.dot(normed_here, query_cols, preferred_element_type=jnp.float32)
        .astype(jnp.bfloat16)
        .reshape(block_shape)
    )
    key_rows = (
        jnp.dot(normed_here, key_cols, preferred_element_type=jnp.float32)
        .astype(jnp.bfloat16)
        .reshape(block_shape)
    )
    value_rows = (
        jnp.dot(normed_here, value_cols, preferred_element_type=jnp.float32)
        .astype(jnp.bfloat16)
        .reshape(block_shape)
    )
    summary = jnp.sum(
        normed_here.reshape(seq_count, nblocks, BL, -1).astype(jnp.float32) * tok_ok[..., None],
        axis=2,
    ) * BL ** (-0.5)

    def plan_of(summary_in, first_in, second_in):
        return sort_plan(summary_in, first_in, second_in, block_ok)

    soft_plan, plan_back = jax.vjp(plan_of, summary, sort_one, sort_two)
    mixed_rows, saved_state = attend_forward(
        queries, key_rows, value_rows, soft_plan, tok_ok, block_ok
    )
    mixed_rows = mixed_rows.reshape(normed_here.shape[0], -1).astype(jnp.bfloat16)
    return (mixed_rows, queries, tok_ok, soft_plan, plan_back, saved_state)


def on_device(
    tokens,
    lengths,
    ln1_gain,
    ln1_bias,
    w_query,
    w_key,
    w_value,
    w_out,
    sort_first,
    sort_second,
    ln2_gain,
    ln2_bias,
    w_up,
    w_down,
    cotangent,
):
    head_side = lax.axis_index("head")
    local_rows = tokens.shape[0]
    inputs = tokens.astype(jnp.float32)
    sort_one = sort_first.astype(jnp.float32)
    sort_two = sort_second.astype(jnp.float32)
    normed_f, norm_back = jax.vjp(layer_norm, inputs, ln1_gain, ln1_bias)
    normed = normed_f.astype(jnp.bfloat16)
    normed_here = lax.all_gather(normed, "head", axis=0, tiled=True)
    query_cols, key_cols, value_cols, out_rows = (w_query, w_key, w_value, w_out)
    sort_share = (head_side == 0).astype(jnp.float32)
    mixed_rows, queries, tok_ok, soft_plan, plan_back, saved_state = run_attention(
        normed_here, lengths, query_cols, key_cols, value_cols, sort_one, sort_two
    )
    attention = lax.psum_scatter(
        jnp.dot(mixed_rows, w_out, preferred_element_type=jnp.float32).astype(jnp.bfloat16),
        "head",
        scatter_dimension=0,
        tiled=True,
    ).astype(jnp.float32)
    middle = inputs + attention
    normed_two_f, norm_two_back = jax.vjp(layer_norm, middle, ln2_gain, ln2_bias)
    normed_two = normed_two_f.astype(jnp.bfloat16)
    up_value = jnp.dot(normed_two, w_up, preferred_element_type=jnp.float32)
    hidden_f, gate_back = jax.vjp(smooth_gate, up_value)
    hidden = hidden_f.astype(jnp.bfloat16)
    output = (middle + jnp.dot(hidden, w_down, preferred_element_type=jnp.float32)).astype(
        jnp.bfloat16
    )
    grad_hidden = jnp.dot(cotangent, w_down.T, preferred_element_type=jnp.float32).astype(
        jnp.bfloat16
    )
    grad_upin = gate_back(grad_hidden.astype(jnp.float32))[0].astype(jnp.bfloat16)
    grad_down = outer_product(hidden, cotangent)
    grad_up = outer_product(normed_two, grad_upin)
    grad_middle_norm, grad_gain_two, grad_bias_two = norm_two_back(
        jnp.dot(grad_upin, w_up.T, preferred_element_type=jnp.float32)
    )
    grad_middle = cotangent.astype(jnp.float32) + grad_middle_norm
    grad_attention = grad_middle.astype(jnp.bfloat16)
    grad_attention_here = lax.all_gather(grad_attention, "head", axis=0, tiled=True)
    grad_w_out = outer_product(mixed_rows, grad_attention_here)
    grad_mixed = jnp.dot(
        grad_attention_here, out_rows.T, preferred_element_type=jnp.float32
    ).astype(jnp.bfloat16)
    grad_queries, grad_keys, grad_values, grad_plan = attend_backward(
        grad_mixed.reshape(queries.shape), queries, soft_plan, tok_ok, saved_state
    )
    grad_plan = lax.psum(grad_plan, "head")
    grad_summary, grad_first, grad_second = plan_back(grad_plan)
    rows_here = normed_here.shape[0]
    grad_queries = grad_queries.reshape(rows_here, -1)
    grad_keys = grad_keys.reshape(rows_here, -1)
    grad_values = grad_values.reshape(rows_here, -1)
    grad_spread = (grad_summary[:, :, None, :] * tok_ok[..., None] * BL ** (-0.5)).reshape(
        rows_here, -1
    )
    grad_w_query = outer_product(normed_here, grad_queries)
    grad_w_key = outer_product(normed_here, grad_keys)
    grad_w_value = outer_product(normed_here, grad_values)
    total_term = jnp.dot(grad_queries, w_query.T, preferred_element_type=jnp.float32)
    total_term = total_term + jnp.dot(grad_keys, w_key.T, preferred_element_type=jnp.float32)
    grad_normed = lax.psum_scatter(
        (total_term + jnp.dot(grad_values, w_value.T, preferred_element_type=jnp.float32)).astype(
            jnp.bfloat16
        ),
        "head",
        scatter_dimension=0,
        tiled=True,
    ).astype(jnp.float32)
    grad_normed = grad_normed + lax.dynamic_slice_in_dim(
        grad_spread, head_side * local_rows, local_rows, 0
    )
    grad_w_query, grad_w_key, grad_w_value, grad_w_out = lax.psum(
        (grad_w_query, grad_w_key, grad_w_value, grad_w_out), "dp"
    )
    grad_inputs_norm, grad_gain_one, grad_bias_one = norm_back(grad_normed)
    input_grad = (grad_middle + grad_inputs_norm).astype(jnp.bfloat16)
    summed = lax.psum(
        (
            grad_gain_one,
            grad_bias_one,
            grad_first * sort_share,
            grad_second * sort_share,
            grad_gain_two,
            grad_bias_two,
            grad_up,
            grad_down,
        ),
        ("dp", "head"),
    )
    return (
        output,
        input_grad,
        summed[0],
        summed[1],
        grad_w_query,
        grad_w_key,
        grad_w_value,
        grad_w_out,
        summed[2],
        summed[3],
        summed[4],
        summed[5],
        summed[6],
        summed[7],
    )


def solution(mesh):
    return jax.shard_map(
        on_device,
        mesh=mesh,
        in_specs=(
            P(("dp", "head"), None),
            P("dp"),
            P(),
            P(),
            P(None, "head"),
            P(None, "head"),
            P(None, "head"),
            P("head", None),
            P(),
            P(),
            P(),
            P(),
            P(),
            P(),
            P(("dp", "head"), None),
        ),
        out_specs=(
            P(("dp", "head"), None),
            P(("dp", "head"), None),
            P(),
            P(),
            P(None, "head"),
            P(None, "head"),
            P(None, "head"),
            P("head", None),
            P(),
            P(),
            P(),
            P(),
            P(),
            P(),
        ),
        check_vma=False,
    )
```

profile of v0, /device:TPU:0, one launch (start us, length us, event | category | flops | bytes accessed | tf_op | source)
XLA Modules:
  0.0 688.6 jit_solution(9410272883061867089)
XLA Ops:
  10.6 2.7 fusion.43
  16.0 33.3 %all-gather.3.cloned.1.call-done = bf16[2048,512]{1,0:T(8,128)(2,1)} async-done(((bf16[1024,512]{1,0:T(8,128)(2,1)}), bf16[2048,512]{1,0:T(8,128)(2,1)}) %all-gather.3.cloned.1.call-update) | async-done | bytes 2097168 | tf_op jit(solution)/shard_map/all_gather | solution.py:183
  49.3 2.9 fusion.17
  67.7 2.7 convolution_convert_fusion.2
  70.4 4.6 reshape.615
  75.0 3.3 convolution_convert_fusion.3
  78.3 4.4 reshape.614
  82.7 2.3 convolution_convert_fusion.4
  85.0 1.8 reshape.613
  86.8 4.9 copy_multiply_fusion.1
  91.7 1.9 convolution_convert_fusion.5
  93.6 1.9 convolution_convert_fusion.6
  95.5 1.9 pad_maximum_fusion
  97.4 2.5 fusion.34
  99.9 2.4 exponential_reduce_fusion
  102.4 2.5 fusion.47
  105.0 2.4 copy.60
  107.4 4.4 convert_element_type.198
  111.8 3.3 convolution_convert_fusion
  115.2 31.9 %reduce-scatter.3.cloned.1.call-done = bf16[1024,512]{1,0:T(8,128)(2,1)} async-done(((bf16[2048,512]{1,0:T(8,128)(2,1)}), bf16[1024,512]{1,0:T(8,128)(2,1)}) %reduce-scatter.3.cloned.1.call-update) | async-done | bytes 1048592 | tf_op jit(solution)/shard_map/reduce_scatter | solution.py:189
  148.7 1.7 multiply_reduce_fusion.3
  150.6 23.5 %multiply_convert_fusion = (bf16[1024,2048]{1,0:T(8,128)(2,1)}, f32[1024,2048]{1,0:T(8,128)S(1)}, f32[1024,2048]{1,0:T(8,128)}) fusion(bf16[512,2048]{1,0:T(8,128)(2,1)S(1)} %copy-done, bf16[1024,512]{1,0:T(8,128)(2,1)S(1)} %copy-done.26, bf16[1024,512]{1,0:T(8,128)(2,1)S(1)} %copy-done.2, f32[512]{0:T(512)} %param.26, f32[512]{0:T(512)} %param.25, ...), kind=kOutput, calls=%fused_computation.12 | convolution fusion | flops 2287992832 | bytes 25178112 | tf_op jit(solution)/shard_map/dot_general | solution.py:198
  174.0 6.9 %fusion.5 = bf16[1024,2048]{1,0:T(8,128)(2,1)S(1)} fusion(f32[1024,2048]{1,0:T(8,128)S(1)} %get-tuple-element.86, f32[1024,2048]{1,0:T(8,128)} %get-tuple-element.110, bf16[1024,512]{1,0:T(8,128)(2,1)S(1)} %copy-done.36, bf16[2048,512]{1,0:T(8,128)(2,1)S(1)} %copy-done.156), kind=kOutput, calls=%fused_computation.8 | convolution fusion | flops 2181038080 | bytes 24117248 | tf_op jit(solution)/shard_map/dot_general | solution.py:204
  180.9 3.3 multiply_reduce_fusion.1
  187.3 6.9 %fusion.167 = f32[2048,512]{1,0:T(8,128)} fusion(bf16[1024,2048]{1,0:T(8,128)(2,1)} %get-tuple-element.85, bf16[1024,512]{1,0:T(8,128)(2,1)} %param.29), kind=kOutput, calls=%fused_computation.381 | convolution fusion | flops 2147483648 | bytes 9437184 | tf_op jit(solution)/shard_map/dot_general | solution.py:41
  194.3 4.6 fusion.143
  198.9 21.4 %all-gather.5.cloned.1.call-done = bf16[2048,512]{1,0:T(8,128)(2,1)} async-done(((bf16[1024,512]{1,0:T(8,128)(2,1)}), bf16[2048,512]{1,0:T(8,128)(2,1)}) %all-gather.5.cloned.1.call-update) | async-done | bytes 2097168 | tf_op jit(solution)/shard_map/all_gather | solution.py:215
  220.3 2.3 convolution_convert_fusion.1
  222.6 1.8 reshape.616
  224.4 3.0 copy_multiply_fusion
  227.5 7.2 %multiply_reduce_fusion = (f32[8,8,4,32]{3,2,1,0:T(4,128)S(1)}, f32[8,8,4,32,64]{4,3,2,1,0:T(8,128)S(1)}) fusion(f32[8,8,4,32,64]{4,3,2,1,0:T(8,128)S(1)} %copy-done.4, f32[8,8,4,32]{3,2,1,0:T(4,128)} %bitcast.104, pred[8,8,32,64]{3,2,1,0:T(8,128)(4,1)S(1)} %broadcast_or_fusion, bf16[8,8,64,4,64]{4,1,3,2,0:T(8,128)(2,1)} %copy-done.35, ...), kind=kOutput, calls=%fused_computation.47 | convolution fusion | flops 69722112 | bytes 7536640 | tf_op jit(solution)/shard_map/cibhd,cikhd->cihbk/dot_general | solution.py:81
  234.7 5.8 convolution_bitcast_fusion
  240.5 2.7 multiply_convert_fusion.2
  246.7 3.1 copy-done.7
  249.8 6.4 fusion.65
  256.2 7.6 %fusion.24 = f32[8,8,32,4,64]{4,1,3,2,0:T(8,128)} fusion(f32[8,8,32,4,64]{4,2,3,1,0:T(8,128)S(1)} %slice.17, f32[8,8,8]{2,1,0:T(8,128)S(1)} %get-tuple-element.88, f32[8,8]{1,0:T(8,128)S(1)} %log_add_fusion.1, f32[8,8]{1,0:T(8,128)S(1)} %log_add_fusion.2), kind=kOutput, calls=%fused_computation.42 | convolution fusion | flops 50332672 | bytes 4196864 | tf_op jit(solution)/shard_map/cij,cithd->cjthd/dot_general | solution.py:105
  263.8 2.4 copy.65
  266.2 3.5 reshape.617
  269.7 2.7 fusion.161
  272.4 3.0 slice.19
  275.5 7.2 %fusion.22 = f32[8,8,32,4,64]{4,1,3,2,0:T(8,128)} fusion(f32[8,8,32,4,64]{4,2,3,1,0:T(8,128)S(1)} %slice.19, f32[8,8,8]{2,1,0:T(8,128)S(1)} %get-tuple-element.88, f32[8,8]{1,0:T(8,128)S(1)} %log_add_fusion.1, f32[8,8]{1,0:T(8,128)S(1)} %log_add_fusion.2), kind=kOutput, calls=%fused_computation.40 | convolution fusion | flops 50332672 | bytes 4196864 | tf_op jit(solution)/shard_map/cij,cithd->cjthd/dot_general | solution.py:108
  282.6 5.5 fusion.75
  288.2 7.2 %psum.91 = f32[8,8,8]{2,1,0:T(8,128)S(1)} all-reduce(f32[8,8,8]{2,1,0:T(8,128)S(1)} %fusion.75), channel_id=1, replica_groups=mesh['dp'=16,'head'=2] {'head'}, use_global_device_ids=true, to_apply=%region_44.45 | all-reduce | flops 512 | bytes 4096 | tf_op jit(solution)/shard_map/psum | solution.py:223
  295.4 12.7 %fusion.14 = (bf16[8,8,32,4,64]{4,2,3,1,0:T(8,128)(2,1)S(1)}, bf16[8,8,32,4,64]{4,2,3,1,0:T(8,128)(2,1)}) fusion(f32[8,8,64,4,64]{4,2,3,1,0:T(8,128)} %convolution_bitcast_fusion, f32[8,8,32,4,64]{4,1,3,2,0:T(8,128)} %fusion.22, f32[8,8,32]{2,1,0:T(8,128)S(1)} %get-tuple-element.101, f32[8,8,32,4,64]{4,1,3,2,0:T(8,128)} %fusion.24, ...), kind=kLoop, calls=%fused_computation.28 | loop fusion | flops 3145728 | bytes 10493952 | tf_op jit(solution)/shard_map/convert_element_type | solution.py:115
  308.4 2.5 copy.75
  310.9 3.5 reshape.619
  318.3 4.1 copy.70
  322.4 3.7 reshape.618
  328.8 2.1 add_convert_fusion
  332.3 3.4 fusion.166
  341.8 2.9 fusion.63
  346.0 6.3 add_convert_fusion.2
  354.0 10.0 %reduce-scatter.5.cloned.1.call-done = bf16[1024,512]{1,0:T(8,128)(2,1)} async-done(((bf16[2048,512]{1,0:T(8,128)(2,1)}), bf16[1024,512]{1,0:T(8,128)(2,1)}) %reduce-scatter.5.cloned.1.call-update) | async-done | bytes 1048592 | tf_op jit(solution)/shard_map/reduce_scatter | solution.py:237
  367.6 40.3 %all-reduce = (f32[512]{0:T(512)}, f32[512]{0:T(512)}, f32[512,8]{0,1:T(8,128)}, f32[512]{0:T(512)}, f32[512]{0:T(512)}) all-reduce(f32[512]{0:T(512)S(1)} %get-tuple-element.16, f32[512]{0:T(512)S(1)} %get-tuple-element.19, f32[512,8]{0,1:T(8,128)S(1)} %fusion.80, ...), channel_id=1, replica_groups=mesh['dp'=16,'head'=2] {'dp','head'}, use_global_device_ids=true, to_apply=%region_96.97 | all-reduce | flops 6144 | bytes 49152 | tf_op jit(solution)/shard_map/psum | solution.py:253
  407.9 3.2 add_convert_fusion.1
  411.1 55.9 %all-reduce.8.cloned.1.call-done = (f32[512,256]{1,0:T(8,128)}, f32[512,256]{1,0:T(8,128)}, f32[512,256]{1,0:T(8,128)}, f32[256,512]{1,0:T(8,128)}) async-done(((f32[512,256]{1,0:T(8,128)}, f32[512,256]{1,0:T(8,128)}, f32[512,256]{1,0:T(8,128)}, f32[256,512]{1,0:T(8,128)}), (f32[512,256]{1,0:T(8,128)}, f32[512,256]{1,0:T(8,128)}, f32[512,256]{1,0:T(8,128)}, ...) | async-done | bytes 2097168 | tf_op jit(solution)/shard_map/psum | solution.py:248
  467.0 198.9 %all-reduce.6.cloned.1.call-done = (f32[512,512]{1,0:T(8,128)}, f32[512,2048]{1,0:T(8,128)}, f32[2048,512]{1,0:T(8,128)}) async-done(((f32[512,512]{1,0:T(8,128)}, f32[512,2048]{1,0:T(8,128)}, f32[2048,512]{1,0:T(8,128)}), (f32[512,512]{1,0:T(8,128)}, f32[512,2048]{1,0:T(8,128)}, f32[2048,512]{1,0:T(8,128)})) %all-reduce.6.cloned.1.call-update) | async-done | bytes 9437200 | tf_op jit(solution)/shard_map/psum | solution.py:253
  665.9 2.0 copy.155
  668.0 1.9 copy.156
  669.8 1.9 copy.157
  671.7 1.9 copy.158
  673.6 2.3 copy.159
  675.8 2.1 copy.160
  679.5 2.0 copy.161
  (484 shorter events, 50.4 us)
Async XLA Ops:
  7.2 143.3 %copy-start = (bf16[512,2048]{1,0:T(8,128)(2,1)S(1)}, bf16[512,2048]{1,0:T(8,128)(2,1)}, u32[]{:S(2)}) copy-start(bf16[512,2048]{1,0:T(8,128)(2,1)} %param.27) | copy-start | bytes 6291460
  7.2 45.0 %copy-start.50 = (bf16[512,512]{1,0:T(8,128)(2,1)S(1)}, bf16[512,512]{1,0:T(8,128)(2,1)}, u32[]{:S(2)}) copy-start(bf16[512,512]{1,0:T(8,128)(2,1)} %param.23) | copy-start | bytes 1572868
  7.2 42.1 %all-gather.3.cloned.1.call-start = ((), (), s32[]{:S(2)}) async-start(), calls=%async_computation.2 | async-start | bytes 3145728 | tf_op jit(solution)/shard_map/all_gather | solution.py:183
  8.9 44.3 %copy-start.149 = (bf16[512,8]{0,1:T(8,128)(2,1)S(1)}, bf16[512,8]{0,1:T(8,128)(2,1)}, u32[]{:S(2)}) copy-start(bf16[512,8]{0,1:T(8,128)(2,1)} %param.24) | copy-start | bytes 24580
  8.9 40.4 %copy-start.68 = (f32[1024]{0:T(1024)}, f32[1024]{0:T(1024)S(1)}, u32[]{:S(2)}) copy-start(f32[1024]{0:T(1024)S(1)} %broadcast_multiply_fusion.1) | copy-start | bytes 12292
  10.6 38.7 %copy-start.111 = (f32[1024]{0:T(1024)}, f32[1024]{0:T(1024)S(1)}, u32[]{:S(2)}) copy-start(f32[1024]{0:T(1024)S(1)} %fusion.45) | copy-start | bytes 12292
  10.6 38.7 %copy-start.107 = (f32[1024]{0:T(1024)}, f32[1024]{0:T(1024)S(1)}, u32[]{:S(2)}) copy-start(f32[1024]{0:T(1024)S(1)} %fusion.127) | copy-start | bytes 12292
  13.3 133.8 %reduce-scatter.3.cloned.1.call-start = ((), (), s32[]{:S(2)}) async-start(), calls=%async_computation.3 | async-start | bytes 3145728 | tf_op jit(solution)/shard_map/reduce_scatter | solution.py:189
  13.5 281.9 %copy-start.48 = (f32[8,8,32]{2,1,0:T(8,128)}, f32[8,8,32]{2,1,0:T(8,128)S(1)}, u32[]{:S(2)}) copy-start(f32[8,8,32]{2,1,0:T(8,128)S(1)} %get-tuple-element.101) | copy-start | bytes 24580
  49.3 18.4 %copy-start.5 = (bf16[2048,512]{1,0:T(8,128)(2,1)S(1)}, bf16[2048,512]{1,0:T(8,128)(2,1)}, u32[]{:S(2)}) copy-start(bf16[2048,512]{1,0:T(8,128)(2,1)} %all-gather.3.cloned.1.call-done) | copy-start | bytes 6291460
  52.6 22.3 %copy-start.52 = (f32[8,8,512]{2,1,0:T(8,128)}, f32[8,8,512]{2,1,0:T(8,128)S(1)}, u32[]{:S(2)}) copy-start(f32[8,8,512]{2,1,0:T(8,128)S(1)} %get-tuple-element.105) | copy-start | bytes 393220
  53.1 21.9 %copy-start.54 = (f32[8,8,512]{2,1,0:T(8,128)}, f32[8,8,512]{2,1,0:T(8,128)S(1)}, u32[]{:S(2)}) copy-start(f32[8,8,512]{2,1,0:T(8,128)S(1)} %fusion.85) | copy-start | bytes 393220
  54.9 8.0 %copy-start.42 = (f32[8,8]{1,0:T(8,128)}, f32[8,8]{1,0:T(8,128)S(1)}, u32[]{:S(2)}) copy-start(f32[8,8]{1,0:T(8,128)S(1)} %log_add_fusion.16) | copy-start | bytes 772
  55.6 10.2 %copy-start.56 = (f32[8,8]{1,0:T(8,128)}, f32[8,8]{1,0:T(8,128)S(1)}, u32[]{:S(2)}) copy-start(f32[8,8]{1,0:T(8,128)S(1)} %log_add_fusion.15) | copy-start | bytes 772
  58.0 16.9 %copy-start.20 = (f32[8,8,8]{2,1,0:T(8,128)}, f32[8,8,8]{2,1,0:T(8,128)S(1)}, u32[]{:S(2)}) copy-start(f32[8,8,8]{2,1,0:T(8,128)S(1)} %get-tuple-element.94) | copy-start | bytes 6148
  61.0 14.0 %copy-start.22 = (f32[8,8,8]{2,1,0:T(8,128)}, f32[8,8,8]{2,1,0:T(8,128)S(1)}, u32[]{:S(2)}) copy-start(f32[8,8,8]{2,1,0:T(8,128)S(1)} %get-tuple-element.92) | copy-start | bytes 6148
  61.6 13.4 %copy-start.46 = (f32[8,8]{1,0:T(8,128)}, f32[8,8]{1,0:T(8,128)S(1)}, u32[]{:S(2)}) copy-start(f32[8,8]{1,0:T(8,128)S(1)} %log_add_fusion.8) | copy-start | bytes 772
  63.6 11.4 %copy-start.37 = (f32[8,8,8]{2,1,0:T(8,128)}, f32[8,8,8]{2,1,0:T(8,128)S(1)}, u32[]{:S(2)}) copy-start(f32[8,8,8]{2,1,0:T(8,128)S(1)} %get-tuple-element.90) | copy-start | bytes 6148
  67.7 7.3 %copy-start.62 = (bf16[512,256]{1,0:T(8,128)(2,1)S(1)}, bf16[512,256]{1,0:T(8,128)(2,1)}, u32[]{:S(2)}) copy-start(bf16[512,256]{1,0:T(8,128)(2,1)} %param.19) | copy-start | bytes 786436
  107.4 39.7 %copy-start.2 = (bf16[1024,512]{1,0:T(8,128)(2,1)S(1)}, bf16[1024,512]{1,0:T(8,128)(2,1)}, u32[]{:S(2)}) copy-start(bf16[1024,512]{1,0:T(8,128)(2,1)} %param.15) | copy-start | bytes 3145732
  115.1 105.2 %all-gather.5.cloned.1.call-start = ((), (), s32[]{:S(2)}) async-start(), calls=%async_computation.4 | async-start | bytes 3145728 | tf_op jit(solution)/shard_map/all_gather | solution.py:215
  150.5 33.8 %copy-start.147 = (f32[1024]{0:T(1024)}, f32[1024]{0:T(1024)S(1)}, u32[]{:S(2)}) copy-start(f32[1024]{0:T(1024)S(1)} %fusion.128) | copy-start | bytes 12292
  150.5 23.5 %copy-start.36 = (bf16[1024,512]{1,0:T(8,128)(2,1)S(1)}, bf16[1024,512]{1,0:T(8,128)(2,1)}, u32[]{:S(2)}) copy-start(bf16[1024,512]{1,0:T(8,128)(2,1)} %param.29) | copy-start | bytes 3145732
  150.5 23.5 %copy-start.156 = (bf16[2048,512]{1,0:T(8,128)(2,1)S(1)}, bf16[2048,512]{1,0:T(8,128)(2,1)}, u32[]{:S(2)}) copy-start(bf16[2048,512]{1,0:T(8,128)(2,1)} %param.28) | copy-start | bytes 6291460
  185.5 8.8 %copy-start.13 = (f32[1024,512]{1,0:T(8,128)}, f32[1024,512]{1,0:T(8,128)S(1)}, u32[]{:S(2)}) copy-start(f32[1024,512]{1,0:T(8,128)S(1)} %get-tuple-element.84) | copy-start | bytes 6291460
  187.0 177.0 %reduce-scatter.5.cloned.1.call-start = ((), (), s32[]{:S(2)}) async-start(), calls=%async_computation.5 | async-start | bytes 3145728 | tf_op jit(solution)/shard_map/reduce_scatter | solution.py:237
  227.4 7.2 %copy-start.40 = (f32[8,4,8,32]{3,2,1,0:T(8,128)S(1)}, f32[8,4,8,32]{3,2,1,0:T(8,128)}, u32[]{:S(2)}) copy-start(f32[8,4,8,32]{3,2,1,0:T(8,128)} %copy-done.39) | copy-start | bytes 98308
  275.5 7.2 %copy-start.9 = (bf16[8,8,32,4,64]{4,1,3,2,0:T(8,128)(2,1)S(1)}, bf16[8,8,32,4,64]{4,1,3,2,0:T(8,128)(2,1)}, u32[]{:S(2)}) copy-start(bf16[8,8,32,4,64]{4,1,3,2,0:T(8,128)(2,1)} %copy-done.8) | copy-start | bytes 3145732
  308.1 7.0 %copy-start.38 = (f32[8,8,8]{2,1,0:T(8,128)S(1)}, f32[8,8,8]{2,1,0:T(8,128)}, u32[]{:S(2)}) copy-start(f32[8,8,8]{2,1,0:T(8,128)} %copy-done.37) | copy-start | bytes 6148
  308.1 7.0 %copy-start.85 = (f32[8,8]{1,0:T(8,128)S(1)}, f32[8,8]{1,0:T(8,128)}, u32[]{:S(2)}) copy-start(f32[8,8]{1,0:T(8,128)} %copy-done.84) | copy-start | bytes 772
  308.1 7.0 %copy-start.100 = (f32[8,8]{1,0:T(8,128)S(1)}, f32[8,8]{1,0:T(8,128)}, u32[]{:S(2)}) copy-start(f32[8,8]{1,0:T(8,128)} %copy-done.99) | copy-start | bytes 772
  308.1 7.4 %copy-start.126 = (f32[8,8]{1,0:T(8,128)S(1)}, f32[8,8]{1,0:T(8,128)}, u32[]{:S(2)}) copy-start(f32[8,8]{1,0:T(8,128)} %copy-done.125) | copy-start | bytes 772
  308.1 7.4 %copy-start.83 = (f32[8,8]{1,0:T(8,128)S(1)}, f32[8,8]{1,0:T(8,128)}, u32[]{:S(2)}) copy-start(f32[8,8]{1,0:T(8,128)} %copy-done.82) | copy-start | bytes 772
  308.1 7.7 %copy-start.140 = (f32[8,8]{1,0:T(8,128)S(1)}, f32[8,8]{1,0:T(8,128)}, u32[]{:S(2)}) copy-start(f32[8,8]{1,0:T(8,128)} %copy-done.139) | copy-start | bytes 772
  308.2 7.7 %copy-start.23 = (f32[8,8,8]{2,1,0:T(8,128)S(1)}, f32[8,8,8]{2,1,0:T(8,128)}, u32[]{:S(2)}) copy-start(f32[8,8,8]{2,1,0:T(8,128)} %copy-done.22) | copy-start | bytes 6148
  308.2 7.7 %copy-start.47 = (f32[8,8]{1,0:T(8,128)S(1)}, f32[8,8]{1,0:T(8,128)}, u32[]{:S(2)}) copy-start(f32[8,8]{1,0:T(8,128)} %copy-done.46) | copy-start | bytes 772
  308.2 7.7 %copy-start.61 = (f32[8,8]{1,0:T(8,128)S(1)}, f32[8,8]{1,0:T(8,128)}, u32[]{:S(2)}) copy-start(f32[8,8]{1,0:T(8,128)} %copy-done.60) | copy-start | bytes 772
  308.2 7.7 %copy-start.91 = (f32[8,8]{1,0:T(8,128)S(1)}, f32[8,8]{1,0:T(8,128)}, u32[]{:S(2)}) copy-start(f32[8,8]{1,0:T(8,128)} %copy-done.90) | copy-start | bytes 772
  308.2 7.7 %copy-start.106 = (f32[8,8]{1,0:T(8,128)S(1)}, f32[8,8]{1,0:T(8,128)}, u32[]{:S(2)}) copy-start(f32[8,8]{1,0:T(8,128)} %copy-done.105) | copy-start | bytes 772
  308.2 8.0 %copy-start.124 = (f32[8,8]{1,0:T(8,128)S(1)}, f32[8,8]{1,0:T(8,128)}, u32[]{:S(2)}) copy-start(f32[8,8]{1,0:T(8,128)} %copy-done.123) | copy-start | bytes 772
  308.2 8.0 %copy-start.75 = (f32[8,8]{1,0:T(8,128)S(1)}, f32[8,8]{1,0:T(8,128)}, u32[]{:S(2)}) copy-start(f32[8,8]{1,0:T(8,128)} %copy-done.74) | copy-start | bytes 772
  308.2 8.3 %copy-start.138 = (f32[8,8]{1,0:T(8,128)S(1)}, f32[8,8]{1,0:T(8,128)}, u32[]{:S(2)}) copy-start(f32[8,8]{1,0:T(8,128)} %copy-done.137) | copy-start | bytes 772
  308.2 8.3 %copy-start.98 = (f32[8,8]{1,0:T(8,128)S(1)}, f32[8,8]{1,0:T(8,128)}, u32[]{:S(2)}) copy-start(f32[8,8]{1,0:T(8,128)} %copy-done.97) | copy-start | bytes 772
  308.2 8.6 %copy-start.122 = (f32[8,8]{1,0:T(8,128)S(1)}, f32[8,8]{1,0:T(8,128)}, u32[]{:S(2)}) copy-start(f32[8,8]{1,0:T(8,128)} %copy-done.121) | copy-start | bytes 772
  308.3 8.7 %copy-start.81 = (f32[8,8]{1,0:T(8,128)S(1)}, f32[8,8]{1,0:T(8,128)}, u32[]{:S(2)}) copy-start(f32[8,8]{1,0:T(8,128)} %copy-done.80) | copy-start | bytes 772
  308.3 8.9 %copy-start.136 = (f32[8,8]{1,0:T(8,128)S(1)}, f32[8,8]{1,0:T(8,128)}, u32[]{:S(2)}) copy-start(f32[8,8]{1,0:T(8,128)} %copy-done.135) | copy-start | bytes 772
  308.3 9.0 %copy-start.21 = (f32[8,8,8]{2,1,0:T(8,128)S(1)}, f32[8,8,8]{2,1,0:T(8,128)}, u32[]{:S(2)}) copy-start(f32[8,8,8]{2,1,0:T(8,128)} %copy-done.20) | copy-start | bytes 6148
  308.3 9.0 %copy-start.45 = (f32[8,8]{1,0:T(8,128)S(1)}, f32[8,8]{1,0:T(8,128)}, u32[]{:S(2)}) copy-start(f32[8,8]{1,0:T(8,128)} %copy-done.44) | copy-start | bytes 772
  308.3 9.0 %copy-start.59 = (f32[8,8]{1,0:T(8,128)S(1)}, f32[8,8]{1,0:T(8,128)}, u32[]{:S(2)}) copy-start(f32[8,8]{1,0:T(8,128)} %copy-done.58) | copy-start | bytes 772
  308.3 9.0 %copy-start.89 = (f32[8,8]{1,0:T(8,128)S(1)}, f32[8,8]{1,0:T(8,128)}, u32[]{:S(2)}) copy-start(f32[8,8]{1,0:T(8,128)} %copy-done.88) | copy-start | bytes 772
  308.3 9.0 %copy-start.104 = (f32[8,8]{1,0:T(8,128)S(1)}, f32[8,8]{1,0:T(8,128)}, u32[]{:S(2)}) copy-start(f32[8,8]{1,0:T(8,128)} %copy-done.103) | copy-start | bytes 772
  308.3 9.3 %copy-start.120 = (f32[8,8]{1,0:T(8,128)S(1)}, f32[8,8]{1,0:T(8,128)}, u32[]{:S(2)}) copy-start(f32[8,8]{1,0:T(8,128)} %copy-done.119) | copy-start | bytes 772
  308.3 9.3 %copy-start.73 = (f32[8,8]{1,0:T(8,128)S(1)}, f32[8,8]{1,0:T(8,128)}, u32[]{:S(2)}) copy-start(f32[8,8]{1,0:T(8,128)} %copy-done.72) | copy-start | bytes 772
  308.4 9.6 %copy-start.134 = (f32[8,8]{1,0:T(8,128)S(1)}, f32[8,8]{1,0:T(8,128)}, u32[]{:S(2)}) copy-start(f32[8,8]{1,0:T(8,128)} %copy-done.133) | copy-start | bytes 772
  308.4 9.6 %copy-start.96 = (f32[8,8]{1,0:T(8,128)S(1)}, f32[8,8]{1,0:T(8,128)}, u32[]{:S(2)}) copy-start(f32[8,8]{1,0:T(8,128)} %copy-done.95) | copy-start | bytes 772
  314.3 12.5 %copy-start.24 = (bf16[2048,256]{1,0:T(8,128)(2,1)}, bf16[2048,256]{1,0:T(8,128)(2,1)S(1)}, u32[]{:S(2)}) copy-start(bf16[2048,256]{1,0:T(8,128)(2,1)S(1)} %reshape.619) | copy-start | bytes 3145732
  316.6 9.5 %copy-start.64 = (bf16[512,256]{1,0:T(8,128)(2,1)S(1)}, bf16[512,256]{1,0:T(8,128)(2,1)}, u32[]{:S(2)}) copy-start(bf16[512,256]{1,0:T(8,128)(2,1)} %param.20) | copy-start | bytes 786436
  330.9 136.2 %all-reduce.8.cloned.1.call-start = ((), (), s32[]{:S(2)}) async-start(), calls=%async_computation.7 | async-start | bytes 4194304 | tf_op jit(solution)/shard_map/psum | solution.py:248
  340.5 325.5 %all-reduce.6.cloned.1.call-start = ((), (), s32[]{:S(2)}) async-start(), calls=%async_computation.6 | async-start | bytes 18874368 | tf_op jit(solution)/shard_map/psum | solution.py:253
  346.0 7.4 %copy-start.51 = (bf16[512,512]{1,0:T(8,128)(2,1)S(1)}, bf16[512,512]{1,0:T(8,128)(2,1)}, u32[]{:S(2)}) copy-start(bf16[512,512]{1,0:T(8,128)(2,1)} %param.23) | copy-start | bytes 1572868
  352.3 12.3 %copy-start.69 = (f32[1024]{0:T(1024)S(1)}, f32[1024]{0:T(1024)}, u32[]{:S(2)}) copy-start(f32[1024]{0:T(1024)} %copy-done.68) | copy-start | bytes 12292
  352.3 12.3 %copy-start.145 = (f32[512]{0:T(512)S(1)}, f32[512]{0:T(512)}, u32[]{:S(2)}) copy-start(f32[512]{0:T(512)} %param.17) | copy-start | bytes 6148
  353.4 11.2 %dynamic-slice-start = ((f32[2048]{0:T(1024)}, s32[]{:T(128)}), f32[1024]{0:T(1024)S(1)}, s32[]{:S(2)}) async-start(f32[2048]{0:T(1024)} %copy-done.146, s32[]{:T(128)} %select_n.18), calls=%async_computation.8 | async-start | bytes 8704 | tf_op jit(solution)/shard_map/dynamic_slice | solution.py:245
  665.9 9.9 %copy-start.34 = (f32[512,2048]{1,0:T(8,128)S(1)}, f32[512,2048]{1,0:T(8,128)}, u32[]{:S(2)}) copy-start(f32[512,2048]{1,0:T(8,128)} %get-tuple-element.128) | copy-start | bytes 12582916
  (103 other events, 293.9 us)
Sparse Core Ops, SparseCore 0:
  13.4 35.8 all-gather.2
  115.2 31.8 reduce-scatter.2
  187.1 33.1 all-gather.4
  331.0 33.0 reduce-scatter.4
  368.4 98.5 all-reduce.7
  474.6 191.2 all-reduce.5
where the time goes:
time: 695 us; the launch traced here: 689 us
  waiting for transfers between devices  352 us (51%)
  matrix products  137 us (20%)
  local copies, waits for them, and re-layouts  75.9 us (11%)
  other arithmetic  58.7 us (8%)
  blocking collectives  47.5 us (7%)
  between operations  17.1 us (2%)
    psum x1, waiting for transfers between devices, on_device(): lax.psum((grad_gain_one, grad_bias_one, grad_first * sort_share, grad_sec...  199 us
    psum x1, waiting for transfers between devices, on_device(): lax.psum((grad_w_query, grad_w_key, grad_w_value, grad_w_out), 'dp')  55.9 us
    psum x1, blocking collectives, on_device(): lax.psum((grad_gain_one, grad_bias_one, grad_first * sort_share, grad_sec...  40.3 us
    all_gather x1, waiting for transfers between devices, on_device(): normed_here = lax.all_gather(normed, 'head', axis=0, tiled=True)  33.3 us
    reduce_scatter x1, waiting for transfers between devices, on_device(): lax.psum_scatter(jnp.dot(mixed_rows, w_out, preferred_element_type=jnp.fl...  31.9 us
    unnamed x327, local copies, waits for them, and re-layouts  31.9 us
    dot_general x1, matrix products, on_device(): up_value = jnp.dot(normed_two, w_up, preferred_element_type=jnp.float32)  23.5 us
    all_gather x1, waiting for transfers between devices, on_device(): lax.all_gather(grad_attention, 'head', axis=0, tiled=True)  21.4 us
  transfers between devices with their start and end apart: 6, of which 6 were waited for; matrix products, arithmetic and copies ran while one was open for 6% of the time, Pallas kernels for 0%

commit v1 on v0

--- a/solution.py
+++ b/solution.py
@@ -251,17 +251,20 @@
     grad_inputs_norm, grad_gain_one, grad_bias_one = norm_back(grad_normed)
     input_grad = (grad_middle + grad_inputs_norm).astype(jnp.bfloat16)
     summed = lax.psum(
-        (
-            grad_gain_one,
-            grad_bias_one,
-            grad_first * sort_share,
-            grad_second * sort_share,
-            grad_gain_two,
-            grad_bias_two,
-            grad_up,
-            grad_down,
+        lax.psum(
+            (
+                grad_gain_one,
+                grad_bias_one,
+                grad_first * sort_share,
+                grad_second * sort_share,
+                grad_gain_two,
+                grad_bias_two,
+                grad_up,
+                grad_down,
+            ),
+            "head",
         ),
-        ("dp", "head"),
+        "dp",
     )
     return (
         output,

time: 695 us -> 815 us (1.17)
  waiting for transfers between devices: 352 us -> 419 us
  blocking collectives: 47.5 us -> 78.2 us
  other arithmetic: 58.7 us -> 78.7 us
    psum x1, waiting for transfers between devices: 55.9 us -> 149 us  [on_device(): lax.psum((grad_w_query, grad_w_key, grad_w_value, grad_w_out), 'dp')]
    psum x0 -> x1, blocking collectives: none -> 63.3 us  [on_device(): lax.psum(lax.psum((grad_gain_one, grad_bias_one, grad_first * sort_share,...]
    psum x1, waiting for transfers between devices: 199 us -> 156 us  [on_device(): lax.psum((grad_gain_one, grad_bias_one, grad_first * sort_share, grad_sec...]
    psum x1, blocking collectives: 40.3 us -> 7.11 us  [on_device(): lax.psum((grad_gain_one, grad_bias_one, grad_first * sort_share, grad_sec...]
    reduce_scatter x1, waiting for transfers between devices: 10 us -> 26.1 us  [on_device(): lax.psum_scatter((total_term + jnp.dot(grad_values, w_value.T, preferred_...]
    div x16, other arithmetic: 0.09 us -> 10.9 us  [log_total(): jnp.log(jnp.sum(jnp.exp(values - row_top), axis=along, keepdims=True))]
    unnamed x327 -> x289, local copies, waits for them, and re-layouts: 31.9 us -> 41.1 us
  transfers between devices with their start and end apart: 6 -> 6, of which waited for: 6 -> 6; matrix products, arithmetic and copies ran while one was open for 6% -> 11% of each run, Pallas kernels for 0% -> 0%
where the time goes in v1:
time: 815 us; the launch traced here: 808 us
  waiting for transfers between devices  419 us (51%)
  matrix products  136 us (17%)
  other arithmetic  78.7 us (10%)
  local copies, waits for them, and re-layouts  78.2 us (10%)
  blocking collectives  78.2 us (10%)
  between operations  16.7 us (2%)
    psum x1, waiting for transfers between devices, on_device(): lax.psum((grad_gain_one, grad_bias_one, grad_first * sort_share, grad_sec...  156 us
    psum x1, waiting for transfers between devices, on_device(): lax.psum((grad_w_query, grad_w_key, grad_w_value, grad_w_out), 'dp')  149 us
    psum x1, blocking collectives, on_device(): lax.psum(lax.psum((grad_gain_one, grad_bias_one, grad_first * sort_share,...  63.3 us
    unnamed x289, local copies, waits for them, and re-layouts  41.1 us
    all_gather x1, waiting for transfers between devices, on_device(): normed_here = lax.all_gather(normed, 'head', axis=0, tiled=True)  34.5 us
    reduce_scatter x1, waiting for transfers between devices, on_device(): lax.psum_scatter(jnp.dot(mixed_rows, w_out, preferred_element_type=jnp.fl...  31.9 us
    reduce_scatter x1, waiting for transfers between devices, on_device(): lax.psum_scatter((total_term + jnp.dot(grad_values, w_value.T, preferred_...  26.1 us
    dot_general x1, matrix products, on_device(): up_value = jnp.dot(normed_two, w_up, preferred_element_type=jnp.float32)  22 us
  transfers between devices with their start and end apart: 6, of which 6 were waited for; matrix products, arithmetic and copies ran while one was open for 11% of the time, Pallas kernels for 0%

profile of v1, /device:TPU:0, one launch (start us, length us, event | category | flops | bytes accessed | tf_op | source)
XLA Modules:
  0.0 807.8 jit_solution(7266030804401634196)
XLA Ops:
  11.8 2.7 fusion.43
  16.0 34.5 %all-gather.3.cloned.1.call-done = bf16[2048,512]{1,0:T(8,128)(2,1)} async-done(((bf16[1024,512]{1,0:T(8,128)(2,1)}), bf16[2048,512]{1,0:T(8,128)(2,1)}) %all-gather.3.cloned.1.call-update) | async-done | bytes 2097168 | tf_op jit(solution)/shard_map/all_gather | solution.py:183
  50.4 2.9 fusion.17
  70.8 2.0 reshape.615
  72.8 2.3 convolution_convert_fusion.3
  75.1 1.8 reshape.614
  76.9 2.3 convolution_convert_fusion.4
  79.2 1.8 reshape.613
  81.0 4.9 copy_multiply_fusion.1
  86.0 1.9 convolution_convert_fusion.5
  87.9 1.9 convolution_convert_fusion.6
  91.5 2.5 fusion.34
  94.0 2.9 exponential_reduce_fusion
  97.0 2.5 fusion.47
  99.5 2.4 copy.60
  101.9 4.4 convert_element_type.198
  106.3 3.3 convolution_convert_fusion
  109.7 31.9 %reduce-scatter.3.cloned.1.call-done = bf16[1024,512]{1,0:T(8,128)(2,1)} async-done(((bf16[2048,512]{1,0:T(8,128)(2,1)}), bf16[1024,512]{1,0:T(8,128)(2,1)}) %reduce-scatter.3.cloned.1.call-update) | async-done | bytes 1048592 | tf_op jit(solution)/shard_map/reduce_scatter | solution.py:189
  145.1 22.0 %multiply_convert_fusion = (bf16[1024,2048]{1,0:T(8,128)(2,1)}, f32[1024,2048]{1,0:T(8,128)S(1)}, f32[1024,2048]{1,0:T(8,128)}) fusion(bf16[512,2048]{1,0:T(8,128)(2,1)S(1)} %copy-done, bf16[1024,512]{1,0:T(8,128)(2,1)S(1)} %copy-done.26, bf16[1024,512]{1,0:T(8,128)(2,1)S(1)} %copy-done.2, f32[512]{0:T(512)S(1)} %copy-done.137, f32[512]{0:T(512)S(1)} %copy-done.129, ...), kind=kOutput, calls=%fused_computation.12 | convolution fusion | flops 2287992832 | bytes 25178112 | tf_op jit(solution)/shard_map/dot_general | solution.py:198
  167.1 6.7 fusion.5
  173.8 3.3 multiply_reduce_fusion.1
  180.6 6.9 fusion.167
  187.6 4.7 fusion.143
  192.2 21.3 %all-gather.5.cloned.1.call-done = bf16[2048,512]{1,0:T(8,128)(2,1)} async-done(((bf16[1024,512]{1,0:T(8,128)(2,1)}), bf16[2048,512]{1,0:T(8,128)(2,1)}) %all-gather.5.cloned.1.call-update) | async-done | bytes 2097168 | tf_op jit(solution)/shard_map/all_gather | solution.py:215
  213.6 2.3 convolution_convert_fusion.1
  215.9 1.8 reshape.616
  217.7 3.0 copy_multiply_fusion
  220.7 8.7 %multiply_reduce_fusion = (f32[8,8,4,32]{3,2,1,0:T(4,128)S(1)}, f32[8,8,4,32,64]{4,3,2,1,0:T(8,128)}) fusion(f32[8,8,4,32,64]{4,3,2,1,0:T(8,128)S(1)} %copy-done.7, f32[8,8,4,32]{3,2,1,0:T(4,128)} %bitcast.104, pred[8,8,32,64]{3,2,1,0:T(8,128)(4,1)S(1)} %broadcast_or_fusion, bf16[8,8,64,4,64]{4,1,3,2,0:T(8,128)(2,1)} %copy-done.34, ...), kind=kOutput, calls=%fused_computation.47 | convolution fusion | flops 69722112 | bytes 7536640 | tf_op jit(solution)/shard_map/cibhd,cikhd->cihbk/dot_general | solution.py:81
  229.4 4.4 convolution_bitcast_fusion
  234.4 3.8 copy-done.8
  239.2 2.7 multiply_convert_fusion.2
  243.8 3.1 copy-done.11
  246.9 2.0 copy-done.4
  248.9 6.4 fusion.65
  255.4 6.6 fusion.75
  262.0 7.8 psum.147
  297.9 3.0 fusion.63
  302.5 3.7 fusion.48
  306.2 2.5 copy.65
  308.7 3.7 reshape.617
  312.4 8.7 %fusion.22 = f32[8,8,32,4,64]{4,1,3,2,0:T(8,128)S(1)} fusion(f32[8,8,32,4,64]{4,2,3,1,0:T(8,128)} %copy-done.3, f32[8,8,8]{2,1,0:T(8,128)S(1)} %get-tuple-element.96, f32[8,8]{1,0:T(8,128)S(1)} %copy-done.57, f32[8,8]{1,0:T(8,128)S(1)} %log_add_fusion.2), kind=kOutput, calls=%fused_computation.40 | convolution fusion | flops 50332672 | bytes 4196864 | tf_op jit(solution)/shard_map/cij,cithd->cjthd/dot_general | solution.py:108
  321.1 6.8 fusion.24
  327.9 11.3 %fusion.14 = (bf16[8,8,32,4,64]{4,2,3,1,0:T(8,128)(2,1)S(1)}, bf16[8,8,32,4,64]{4,2,3,1,0:T(8,128)(2,1)}) fusion(f32[8,8,64,4,64]{4,2,3,1,0:T(8,128)} %copy-done.8, f32[8,8,32,4,64]{4,1,3,2,0:T(8,128)S(1)} %fusion.22, f32[8,8,32]{2,1,0:T(8,128)S(1)} %copy-done.43, f32[8,8,32,4,64]{4,1,3,2,0:T(8,128)S(1)} %fusion.24, f32[8,8,64,4,64]{4,2,3,1,0:T(8,128)} %copy-done.11), kind=kLoop, calls=%fused_computation.28 | loop fusion | flops 3145728 | bytes 10493952 | tf_op jit(solution)/shard_map/convert_element_type | solution.py:115
  339.2 2.5 copy.75
  341.6 4.3 reshape.619
  346.0 4.1 copy.70
  350.1 3.5 reshape.618
  353.6 2.0 fusion.161
  356.9 2.1 add_convert_fusion
  359.3 3.6 fusion.166
  367.5 156.4 %all-reduce.9.cloned.1.call-done = (f32[512,512]{1,0:T(8,128)}, f32[512,2048]{1,0:T(8,128)}, f32[2048,512]{1,0:T(8,128)}) async-done(((f32[512,512]{1,0:T(8,128)}, f32[512,2048]{1,0:T(8,128)}, f32[2048,512]{1,0:T(8,128)}), (f32[512,512]{1,0:T(8,128)}, f32[512,2048]{1,0:T(8,128)}, f32[2048,512]{1,0:T(8,128)})) %all-reduce.9.cloned.1.call-update) | async-done | bytes 9437200 | tf_op jit(solution)/shard_map/psum | solution.py:254
  525.2 6.3 add_convert_fusion.2
  532.5 26.1 %reduce-scatter.5.cloned.1.call-done = bf16[1024,512]{1,0:T(8,128)(2,1)} async-done(((bf16[2048,512]{1,0:T(8,128)(2,1)}), bf16[1024,512]{1,0:T(8,128)(2,1)}) %reduce-scatter.5.cloned.1.call-update) | async-done | bytes 1048592 | tf_op jit(solution)/shard_map/reduce_scatter | solution.py:237
  562.1 7.1 all-reduce.2
  569.2 63.3 %all-reduce = (f32[512]{0:T(512)}, f32[512]{0:T(512)}, f32[512,8]{0,1:T(8,128)}, f32[512]{0:T(512)}, f32[512]{0:T(512)}) all-reduce(f32[512]{0:T(512)S(1)} %get-tuple-element.68, f32[512]{0:T(512)S(1)} %get-tuple-element.69, f32[512,8]{0,1:T(8,128)S(1)} %get-tuple-element.70, ...), channel_id=1, replica_groups=mesh['dp'=16,'head'=2] {'dp'}, use_global_device_ids=true, to_apply=%region_97.98 | all-reduce | flops 6144 | bytes 49152 | tf_op jit(solution)/shard_map/psum | solution.py:253
  632.5 3.3 add_convert_fusion.1
  635.8 149.1 %all-reduce.7.cloned.1.call-done = (f32[512,256]{1,0:T(8,128)}, f32[512,256]{1,0:T(8,128)}, f32[512,256]{1,0:T(8,128)}, f32[256,512]{1,0:T(8,128)}, f32[512,512]...) async-done(((f32[512,256]{1,0:T(8,128)}, f32[512,256]{1,0:T(8,128)}, f32[512,256]{1,0:T(8,128)}, f32[256,512]{1,0:T(8,128)}, f32[512,512]{1,0:T(8,128)}, ...) | async-done | bytes 11534352 | tf_op jit(solution)/shard_map/psum | solution.py:248
  784.9 2.0 copy.158
  786.9 1.9 copy.159
  788.8 1.9 copy.160
  790.7 1.9 copy.161
  792.5 2.3 copy.162
  794.8 2.1 copy.163
  798.5 2.0 copy.164
  (447 shorter events, 77.7 us)
Async XLA Ops:
  7.2 137.9 %copy-start = (bf16[512,2048]{1,0:T(8,128)(2,1)S(1)}, bf16[512,2048]{1,0:T(8,128)(2,1)}, u32[]{:S(2)}) copy-start(bf16[512,2048]{1,0:T(8,128)(2,1)} %param.27) | copy-start | bytes 6291460
  7.2 7.3 copy-start.131
  7.2 46.1 %copy-start.44 = (bf16[512,512]{1,0:T(8,128)(2,1)S(1)}, bf16[512,512]{1,0:T(8,128)(2,1)}, u32[]{:S(2)}) copy-start(bf16[512,512]{1,0:T(8,128)(2,1)} %param.23) | copy-start | bytes 1572868
  7.2 43.2 %all-gather.3.cloned.1.call-start = ((), (), s32[]{:S(2)}) async-start(), calls=%async_computation.2 | async-start | bytes 3145728 | tf_op jit(solution)/shard_map/all_gather | solution.py:183
  8.9 45.4 %copy-start.126 = (bf16[512,8]{0,1:T(8,128)(2,1)S(1)}, bf16[512,8]{0,1:T(8,128)(2,1)}, u32[]{:S(2)}) copy-start(bf16[512,8]{0,1:T(8,128)(2,1)} %param.24) | copy-start | bytes 24580
  14.5 127.2 %reduce-scatter.3.cloned.1.call-start = ((), (), s32[]{:S(2)}) async-start(), calls=%async_computation.3 | async-start | bytes 3145728 | tf_op jit(solution)/shard_map/reduce_scatter | solution.py:189
  14.6 52.8 %copy-start.41 = (f32[8,8,32]{2,1,0:T(8,128)}, f32[8,8,32]{2,1,0:T(8,128)S(1)}, u32[]{:S(2)}) copy-start(f32[8,8,32]{2,1,0:T(8,128)S(1)} %get-tuple-element.109) | copy-start | bytes 24580
  15.4 49.1 %copy-start.134 = (pred[8,8]{1,0:T(8,128)(4,1)}, pred[8,8]{1,0:T(8,128)(4,1)S(1)}, u32[]{:S(2)}) copy-start(pred[8,8]{1,0:T(8,128)(4,1)S(1)} %iota_compare_fusion) | copy-start | bytes 196
  15.4 39.1 %copy-start.122 = (pred[8,8]{1,0:T(8,128)(4,1)}, pred[8,8]{1,0:T(8,128)(4,1)S(1)}, u32[]{:S(2)}) copy-start(pred[8,8]{1,0:T(8,128)(4,1)S(1)} %get-tuple-element.111) | copy-start | bytes 196
  15.4 48.6 %copy-start.127 = (pred[8,8]{1,0:T(8,128)(4,1)}, pred[8,8]{1,0:T(8,128)(4,1)S(1)}, u32[]{:S(2)}) copy-start(pred[8,8]{1,0:T(8,128)(4,1)S(1)} %get-tuple-element.112) | copy-start | bytes 196
  50.4 18.7 %copy-start.9 = (bf16[2048,512]{1,0:T(8,128)(2,1)S(1)}, bf16[2048,512]{1,0:T(8,128)(2,1)}, u32[]{:S(2)}) copy-start(bf16[2048,512]{1,0:T(8,128)(2,1)} %all-gather.3.cloned.1.call-done) | copy-start | bytes 6291460
  53.8 13.7 %copy-start.46 = (f32[8,8,512]{2,1,0:T(8,128)}, f32[8,8,512]{2,1,0:T(8,128)S(1)}, u32[]{:S(2)}) copy-start(f32[8,8,512]{2,1,0:T(8,128)S(1)} %get-tuple-element.113) | copy-start | bytes 393220
  54.3 13.2 %copy-start.48 = (f32[8,8,512]{2,1,0:T(8,128)}, f32[8,8,512]{2,1,0:T(8,128)S(1)}, u32[]{:S(2)}) copy-start(f32[8,8,512]{2,1,0:T(8,128)S(1)} %fusion.85) | copy-start | bytes 393220
  101.9 39.7 %copy-start.2 = (bf16[1024,512]{1,0:T(8,128)(2,1)S(1)}, bf16[1024,512]{1,0:T(8,128)(2,1)}, u32[]{:S(2)}) copy-start(bf16[1024,512]{1,0:T(8,128)(2,1)} %param.15) | copy-start | bytes 3145732
  109.6 103.9 %all-gather.5.cloned.1.call-start = ((), (), s32[]{:S(2)}) async-start(), calls=%async_computation.4 | async-start | bytes 3145728 | tf_op jit(solution)/shard_map/all_gather | solution.py:215
  143.3 33.8 %copy-start.118 = (f32[1024]{0:T(1024)}, f32[1024]{0:T(1024)S(1)}, u32[]{:S(2)}) copy-start(f32[1024]{0:T(1024)S(1)} %broadcast_multiply_fusion) | copy-start | bytes 12292
  145.1 32.0 %copy-start.124 = (f32[1024]{0:T(1024)}, f32[1024]{0:T(1024)S(1)}, u32[]{:S(2)}) copy-start(f32[1024]{0:T(1024)S(1)} %fusion.128) | copy-start | bytes 12292
  145.1 22.0 %copy-start.35 = (bf16[1024,512]{1,0:T(8,128)(2,1)S(1)}, bf16[1024,512]{1,0:T(8,128)(2,1)}, u32[]{:S(2)}) copy-start(bf16[1024,512]{1,0:T(8,128)(2,1)} %param.29) | copy-start | bytes 3145732
  145.1 22.0 %copy-start.136 = (bf16[2048,512]{1,0:T(8,128)(2,1)S(1)}, bf16[2048,512]{1,0:T(8,128)(2,1)}, u32[]{:S(2)}) copy-start(bf16[2048,512]{1,0:T(8,128)(2,1)} %param.28) | copy-start | bytes 6291460
  178.3 9.2 %copy-start.16 = (f32[1024,512]{1,0:T(8,128)}, f32[1024,512]{1,0:T(8,128)S(1)}, u32[]{:S(2)}) copy-start(f32[1024,512]{1,0:T(8,128)S(1)} %get-tuple-element.92) | copy-start | bytes 6291460
  180.3 343.6 %all-reduce.9.cloned.1.call-start = ((), (), s32[]{:S(2)}) async-start(), calls=%async_computation.7 | async-start | bytes 18874368 | tf_op jit(solution)/shard_map/psum | solution.py:254
  180.5 7.0 copy-start.27
  180.5 7.0 copy-start.119
  180.5 7.0 copy-start.125
  180.5 7.0 copy-start.130
  180.6 7.0 copy-start.138
  180.6 7.0 copy-start.140
  220.7 8.7 %copy-start.39 = (f32[8,4,8,32]{3,2,1,0:T(8,128)S(1)}, f32[8,4,8,32]{3,2,1,0:T(8,128)}, u32[]{:S(2)}) copy-start(f32[8,4,8,32]{3,2,1,0:T(8,128)} %copy-done.38) | copy-start | bytes 98308
  238.1 17.1 %copy-start.3 = (f32[8,8,32,4,64]{4,2,3,1,0:T(8,128)}, f32[8,8,32,4,64]{4,2,3,1,0:T(8,128)S(1)}, u32[]{:S(2)}) copy-start(f32[8,8,32,4,64]{4,2,3,1,0:T(8,128)S(1)} %slice.19) | copy-start | bytes 6291460
  248.9 6.4 copy-start.13
  255.3 14.5 %copy-start.57 = (f32[8,8]{1,0:T(8,128)S(1)}, f32[8,8]{1,0:T(8,128)}, u32[]{:S(2)}) copy-start(f32[8,8]{1,0:T(8,128)} %log_add_fusion.1) | copy-start | bytes 772
  255.3 15.3 %copy-start.61 = (f32[8,8]{1,0:T(8,128)S(1)}, f32[8,8]{1,0:T(8,128)}, u32[]{:S(2)}) copy-start(f32[8,8]{1,0:T(8,128)} %copy-done.60) | copy-start | bytes 772
  255.3 16.3 %copy-start.71 = (f32[8,8]{1,0:T(8,128)S(1)}, f32[8,8]{1,0:T(8,128)}, u32[]{:S(2)}) copy-start(f32[8,8]{1,0:T(8,128)} %copy-done.70) | copy-start | bytes 772
  255.3 17.3 %copy-start.37 = (f32[8,8,8]{2,1,0:T(8,128)S(1)}, f32[8,8,8]{2,1,0:T(8,128)}, u32[]{:S(2)}) copy-start(f32[8,8,8]{2,1,0:T(8,128)} %copy-done.36) | copy-start | bytes 6148
  255.3 17.2 %copy-start.77 = (f32[8,8]{1,0:T(8,128)S(1)}, f32[8,8]{1,0:T(8,128)}, u32[]{:S(2)}) copy-start(f32[8,8]{1,0:T(8,128)} %copy-done.76) | copy-start | bytes 772
  255.3 17.2 %copy-start.89 = (f32[8,8]{1,0:T(8,128)S(1)}, f32[8,8]{1,0:T(8,128)}, u32[]{:S(2)}) copy-start(f32[8,8]{1,0:T(8,128)} %copy-done.88) | copy-start | bytes 772
  255.3 18.2 %copy-start.75 = (f32[8,8]{1,0:T(8,128)S(1)}, f32[8,8]{1,0:T(8,128)}, u32[]{:S(2)}) copy-start(f32[8,8]{1,0:T(8,128)} %copy-done.74) | copy-start | bytes 772
  255.4 19.2 %copy-start.55 = (f32[8,8]{1,0:T(8,128)S(1)}, f32[8,8]{1,0:T(8,128)}, u32[]{:S(2)}) copy-start(f32[8,8]{1,0:T(8,128)} %copy-done.54) | copy-start | bytes 772
  255.4 19.2 %copy-start.81 = (f32[8,8]{1,0:T(8,128)S(1)}, f32[8,8]{1,0:T(8,128)}, u32[]{:S(2)}) copy-start(f32[8,8]{1,0:T(8,128)} %copy-done.80) | copy-start | bytes 772
  255.4 19.2 %copy-start.93 = (f32[8,8]{1,0:T(8,128)S(1)}, f32[8,8]{1,0:T(8,128)}, u32[]{:S(2)}) copy-start(f32[8,8]{1,0:T(8,128)} %copy-done.92) | copy-start | bytes 772
  255.4 20.9 %copy-start.69 = (f32[8,8]{1,0:T(8,128)S(1)}, f32[8,8]{1,0:T(8,128)}, u32[]{:S(2)}) copy-start(f32[8,8]{1,0:T(8,128)} %copy-done.68) | copy-start | bytes 772
  255.4 26.6 %copy-start.53 = (f32[8,8]{1,0:T(8,128)S(1)}, f32[8,8]{1,0:T(8,128)}, u32[]{:S(2)}) copy-start(f32[8,8]{1,0:T(8,128)} %copy-done.52) | copy-start | bytes 772
  255.4 29.0 %copy-start.67 = (f32[8,8]{1,0:T(8,128)S(1)}, f32[8,8]{1,0:T(8,128)}, u32[]{:S(2)}) copy-start(f32[8,8]{1,0:T(8,128)} %copy-done.66) | copy-start | bytes 772
  255.4 34.6 %copy-start.51 = (f32[8,8]{1,0:T(8,128)S(1)}, f32[8,8]{1,0:T(8,128)}, u32[]{:S(2)}) copy-start(f32[8,8]{1,0:T(8,128)} %copy-done.50) | copy-start | bytes 772
  255.4 37.0 %copy-start.65 = (f32[8,8]{1,0:T(8,128)S(1)}, f32[8,8]{1,0:T(8,128)}, u32[]{:S(2)}) copy-start(f32[8,8]{1,0:T(8,128)} %copy-done.64) | copy-start | bytes 772
  255.4 41.2 %copy-start.47 = (f32[8,8,512]{2,1,0:T(8,128)S(1)}, f32[8,8,512]{2,1,0:T(8,128)}, u32[]{:S(2)}) copy-start(f32[8,8,512]{2,1,0:T(8,128)} %copy-done.46) | copy-start | bytes 393220
  300.9 257.6 %reduce-scatter.5.cloned.1.call-start = ((), (), s32[]{:S(2)}) async-start(), calls=%async_computation.5 | async-start | bytes 3145728 | tf_op jit(solution)/shard_map/reduce_scatter | solution.py:237
  312.3 41.2 %copy-start.20 = (bf16[2048,256]{1,0:T(8,128)(2,1)}, bf16[2048,256]{1,0:T(8,128)(2,1)S(1)}, u32[]{:S(2)}) copy-start(bf16[2048,256]{1,0:T(8,128)(2,1)S(1)} %reshape.617) | copy-start | bytes 3145732
  312.4 8.7 %copy-start.5 = (f32[8,8,32,4,64]{4,2,3,1,0:T(8,128)S(1)}, f32[8,8,32,4,64]{4,2,3,1,0:T(8,128)}, u32[]{:S(2)}) copy-start(f32[8,8,32,4,64]{4,2,3,1,0:T(8,128)} %copy-done.4) | copy-start | bytes 6291460
  321.1 6.8 copy-start.43
  359.0 426.0 %all-reduce.7.cloned.1.call-start = ((), (), s32[]{:S(2)}) async-start(), calls=%async_computation.6 | async-start | bytes 23068672 | tf_op jit(solution)/shard_map/psum | solution.py:248
  524.0 7.4 copy-start.121
  525.1 6.3 copy-start.49
  525.1 6.3 copy-start.97
  525.1 6.3 copy-start.123
  525.1 6.3 copy-start.128
  525.2 6.3 copy-start.135
  525.2 6.7 copy-start.45
  525.2 6.7 copy-start.84
  531.5 27.6 %copy-start.63 = (f32[1024]{0:T(1024)S(1)}, f32[1024]{0:T(1024)}, u32[]{:S(2)}) copy-start(f32[1024]{0:T(1024)} %copy-done.62) | copy-start | bytes 12292
  531.5 27.6 %copy-start.120 = (f32[512]{0:T(512)S(1)}, f32[512]{0:T(512)}, u32[]{:S(2)}) copy-start(f32[512]{0:T(512)} %param.17) | copy-start | bytes 6148
  531.8 27.3 %dynamic-slice-start = ((f32[2048]{0:T(1024)}, s32[]{:T(128)}), f32[1024]{0:T(1024)S(1)}, s32[]{:S(2)}) async-start(f32[2048]{0:T(1024)} %copy-done.121, s32[]{:T(128)} %select_n.18), calls=%async_computation.8 | async-start | bytes 8704 | tf_op jit(solution)/shard_map/dynamic_slice | solution.py:245
  559.8 72.7 %copy-start.99 = (f32[1024]{0:T(1024)S(1)}, f32[1024]{0:T(1024)}, u32[]{:S(2)}) copy-start(f32[1024]{0:T(1024)} %copy-done.98) | copy-start | bytes 12292
  784.9 9.9 %copy-start.32 = (f32[512,2048]{1,0:T(8,128)S(1)}, f32[512,2048]{1,0:T(8,128)}, u32[]{:S(2)}) copy-start(f32[512,2048]{1,0:T(8,128)} %get-tuple-element.136) | copy-start | bytes 12582916
  (84 other events, 188.5 us)
Sparse Core Ops, SparseCore 0:
  14.6 35.8 all-gather.2
  109.8 31.8 reduce-scatter.2
  180.4 33.1 all-gather.4
  301.0 222.8 all-reduce.8
  526.7 31.8 reduce-scatter.4
  563.8 221.1 all-reduce.6
